TPU v7x, 32 devices: a whole 2x2x4 slice. The times are simulated.
32 devices in a mesh: replica: 8 (over z, core), shard: 4 (over y, x).
Axes of the slice: x: 2, y: 2, z: 4, core: 2. Of those that a mesh axis runs over, the one named last changes fastest.
Arguments:
- local_weights: bfloat16 [8, 8192, 512], P('replica', 'shard'), may hold values from -1.3258252 to 1.3258252
- outer_base: bfloat16 [8192, 512], P('shard'), may hold values from -0.0625 to 0.0625
- momentum: bfloat16 [8192, 512], P('shard', 'replica'), may hold values from -0.06591797 to 0.06591797
- error_feedback: bfloat16 [8, 8192, 512], P('replica', 'shard'), may hold values from -0.032958984 to 0.032958984
- q_start: float32 [512, 32], replicated, may hold values from -6 to 6
- tokens: bfloat16 [8, 512, 8192], P('replica', None, 'shard'), may hold values from -6 to 6
Outputs:
- new_base: bfloat16 [8192, 512], P('shard')
- new_momentum: bfloat16 [8192, 512], P('shard', 'replica')
- new_error: bfloat16 [8, 8192, 512], P('replica', 'shard')
- key_rows: bfloat16 [8, 512, 512], P('replica', 'shard')
All inputs are finite; a program needn't handle non-finite values.
Results may differ from a plain program's by a relative error of at most 0.0065.
Values may be sent and summed in bfloat16 or wider, within the bound.
A program may use at most 64 MiB of HBM per device.

v0:
```python
import jax
import jax.numpy as jnp
from jax import lax
from jax.sharding import PartitionSpec as P

outer_mu = 0.9
outer_rate = 0.7


def on_device(local_weights, outer_base, momentum, error_feedback, q_start, tokens):
    highest = lax.Precision.HIGHEST
    replicas = lax.axis_size("replica")
    own_columns = momentum.shape[1]
    full_momentum = lax.all_gather(momentum, "replica", axis=1, tiled=True)
    pseudo = (
        outer_base.astype(jnp.float32)
        - local_weights[0].astype(jnp.float32)
        + error_feedback[0].astype(jnp.float32)
    )
    p_local = jnp.dot(pseudo, q_start, precision=highest)
    p_mean = lax.psum(p_local, "replica") / replicas
    own_gram = jnp.dot(p_mean.T, p_mean, precision=highest)
    gram_sum = lax.psum(own_gram, "shard")
    factor_low = jnp.linalg.cholesky(gram_sum)
    basis = jax.scipy.linalg.solve_triangular(factor_low, p_mean.T, lower=True).T
    q_raw = jnp.dot(pseudo.T, basis, precision=highest)
    q_mean = lax.psum(q_raw, ("replica", "shard")) / replicas
    update = jnp.dot(basis, q_mean.T, precision=highest)
    new_error = (pseudo - update).astype(jnp.bfloat16)[None]
    moment = outer_mu * full_momentum.astype(jnp.float32) + update
    new_base = (outer_base.astype(jnp.float32) - outer_rate * (outer_mu * moment + update)).astype(
        jnp.bfloat16
    )
    first_column = lax.axis_index("replica") * own_columns
    new_momentum = lax.dynamic_slice_in_dim(moment, first_column, own_columns, 1).astype(
        jnp.bfloat16
    )
    own_tokens = tokens[0]
    key_sum = lax.psum_scatter(
        jnp.dot(own_tokens, new_base, preferred_element_type=jnp.float32),
        "shard",
        scatter_dimension=0,
        tiled=True,
    )
    key_rows = key_sum.astype(jnp.bfloat16)[None]
    return (new_base, new_momentum, new_error, key_rows)


def solution(mesh):
    in_specs = (
        P("replica", "shard", None),
        P("shard", None),
        P("shard", "replica"),
        P("replica", "shard", None),
        P(),
        P("replica", None, "shard"),
    )
    out_specs = (
        P("shard", None),
        P("shard", "replica"),
        P("replica", "shard", None),
        P("replica", "shard", None),
    )
    return jax.shard_map(
        on_device, mesh=mesh, in_specs=in_specs, out_specs=out_specs, check_vma=False
    )
```

profile of v0, /device:TPU:0, one launch (start us, length us, event | category | flops | bytes accessed | tf_op | source)
XLA Modules:
  0.0 319.2 jit_solution(3947755793024692435)
XLA Ops:
  7.2 0.0 copy-start
  7.2 0.0 all-reduce.3.cloned.1.call-start
  7.2 4.1 %copy.10 = bf16[2048,512]{0,1:T(8,128)(2,1)} copy(bf16[2048,512]{1,0:T(8,128)(2,1)} %param.7) | data formatting | bytes 4194304 | tf_op args[1]
  11.3 4.0 %copy.11 = bf16[1,2048,512]{1,2,0:T(8,128)(2,1)} copy(bf16[1,2048,512]{2,1,0:T(8,128)(2,1)} %param.6) | data formatting | bytes 4194304 | tf_op args[0]
  15.3 0.0 copy-start.6
  15.3 3.9 %copy.12 = bf16[1,2048,512]{1,2,0:T(8,128)(2,1)} copy(bf16[1,2048,512]{2,1,0:T(8,128)(2,1)} %param.9) | data formatting | bytes 4194304 | tf_op args[3]
  19.2 0.0 copy-done.6
  19.2 6.8 %fusion.10 = f32[2048,32]{0,1:T(8,128)} fusion(f32[512,32]{0,1:T(8,128)S(1)} %copy-done.6, bf16[2048,512]{0,1:T(8,128)(2,1)} %copy.10, bf16[1,2048,512]{1,2,0:T(8,128)(2,1)} %copy.12, bf16[1,2048,512]{1,2,0:T(8,128)(2,1)} %copy.11), kind=kOutput, calls=%fused_computation.11 | convolution fusion | flops 407896064 | bytes 6619136 | tf_op jit(solution)/shard_map/dot_general | solution.py:20
  26.0 0.0 all-reduce.3.cloned.1.call-update
  26.0 0.0 all-reduce.5.cloned.1.call-start
  26.1 58.3 %all-reduce.3.cloned.1.call-done = f32[2048,32]{0,1:T(8,128)} async-done(((f32[2048,32]{0,1:T(8,128)}), f32[2048,32]{0,1:T(8,128)}) %all-reduce.3.cloned.1.call-update) | async-done | bytes 262160 | tf_op jit(solution)/shard_map/psum | solution.py:21
  84.3 1.4 fusion.16
  85.7 16.0 %psum.22 = f32[32,32]{0,1:T(8,128)S(1)} all-reduce(f32[32,32]{0,1:T(8,128)S(1)} %fusion.16), channel_id=1, replica_groups=mesh['replica'=8,'shard'=4] {'shard'}, use_global_device_ids=true, to_apply=%region_1.0 | all-reduce | flops 1024 | bytes 8192 | tf_op jit(solution)/shard_map/psum | solution.py:23
  101.7 0.1 copy.14
  101.8 2.9 cholesky.16
  104.7 0.6 compare_reduce_fusion
  105.4 0.7 fusion.21
  106.0 2.4 custom-call.7
  108.4 1.4 fusion.14
  109.8 6.4 %fusion.8 = f32[512,32]{1,0:T(8,128)} fusion(f32[32,2048]{1,0:T(8,128)S(1)} %fusion.14, bf16[2048,512]{0,1:T(8,128)(2,1)} %copy.10, bf16[1,2048,512]{1,2,0:T(8,128)(2,1)} %copy.12, bf16[1,2048,512]{1,2,0:T(8,128)(2,1)} %copy.11), kind=kOutput, calls=%fused_computation.10 | convolution fusion | flops 407896064 | bytes 6619136 | tf_op jit(solution)/shard_map/dot_general | solution.py:26
  116.2 0.0 all-reduce.5.cloned.1.call-update
  116.3 0.0 all-gather.2.cloned.1.call-start
  116.3 0.7 all-gather.2.cloned.1.call-update
  117.0 0.2 reduce-scatter.2.cloned.1.call-start
  117.2 123.0 %all-reduce.5.cloned.1.call-done = f32[512,32]{1,0:T(8,128)} async-done(((f32[512,32]{1,0:T(8,128)}), f32[512,32]{1,0:T(8,128)}) %all-reduce.5.cloned.1.call-update) | async-done | bytes 65552 | tf_op jit(solution)/shard_map/psum | solution.py:27
  240.2 29.8 %all-gather.2.cloned.1.call-done = bf16[2048,512]{0,1:T(8,128)(2,1)} async-done(((bf16[2048,64]{0,1:T(8,128)(2,1)}), bf16[2048,512]{0,1:T(8,128)(2,1)}) %all-gather.2.cloned.1.call-update) | async-done | bytes 2097168 | tf_op jit(solution)/shard_map/all_gather | solution.py:14
  270.1 0.0 copy-start.1
  270.1 0.0 copy-start.2
  270.1 0.0 copy-start.3
  270.1 0.0 copy-start.4
  270.1 6.3 %multiply_add_fusion = (bf16[2048,512]{0,1:T(8,128)(2,1)}, f32[2048,512]{0,1:T(8,128)S(1)}) fusion(bf16[2048,512]{0,1:T(8,128)(2,1)} %all-gather.2.cloned.1.call-done, f32[32,2048]{1,0:T(8,128)S(1)} %fusion.14, f32[512,32]{1,0:T(8,128)} %all-reduce.5.cloned.1.call-done), kind=kOutput, calls=%fused_computation.5 | convolution fusion | flops 406863872 | bytes 8716288 | tf_op jit(solution)/shard_map/dot_general | solution.py:28
  276.4 0.0 copy-done.1
  276.4 0.0 copy-done.2
  276.4 0.0 copy-done.3
  276.4 0.0 copy-done.4
  276.4 3.5 %fusion.2 = (bf16[1,2048,512]{1,2,0:T(8,128)(2,1)}, bf16[2048,512]{0,1:T(8,128)(2,1)S(1)}) fusion(f32[2048,512]{0,1:T(8,128)S(1)} %get-tuple-element.11, bf16[1,2048,512]{1,2,0:T(8,128)(2,1)S(1)} %copy-done.3, bf16[1,2048,512]{1,2,0:T(8,128)(2,1)S(1)} %copy-done.2, bf16[2048,512]{0,1:T(8,128)(2,1)S(1)} %copy-done.1, bf16[2048,512]{0,1:T(8,128)(2,1)S(1)} %copy-done.4), kind=kLoop, calls=%fused_computation.6 | loop fusion | flops 15728640 | bytes 16777216 | tf_op jit(solution)/shard_map/broadcast_in_dim | solution.py:29
  279.8 0.0 copy-start.5
  279.9 1.3 copy-done.5
  281.2 0.0 copy-done
  281.2 2.3 fusion.5
  283.4 0.0 reduce-scatter.2.cloned.1.call-update
  283.5 3.9 %copy.15 = bf16[2048,512]{1,0:T(8,128)(2,1)} copy(bf16[2048,512]{0,1:T(8,128)(2,1)} %copy-done.5) | data formatting | bytes 4194304
  287.4 4.0 %copy.16 = bf16[1,2048,512]{2,1,0:T(8,128)(2,1)} copy(bf16[1,2048,512]{1,2,0:T(8,128)(2,1)} %get-tuple-element.8) | data formatting | bytes 4194304
  291.3 1.7 dynamic-slice_convert_fusion
  293.0 17.9 %reduce-scatter.2.cloned.1.call-done = f32[128,512]{0,1:T(8,128)} async-done(((f32[512,512]{0,1:T(8,128)}), f32[128,512]{0,1:T(8,128)}) %reduce-scatter.2.cloned.1.call-update) | async-done | bytes 262160 | tf_op jit(solution)/shard_map/reduce_scatter | solution.py:39
  310.9 1.0 convert_bitcast_fusion
  311.9 0.8 copy.17
  (2 shorter events, 0.0 us)
Async XLA Ops:
  7.2 274.0 %copy-start = (bf16[1,512,2048]{2,1,0:T(8,128)(2,1)S(1)}, bf16[1,512,2048]{2,1,0:T(8,128)(2,1)}, u32[]{:S(2)}) copy-start(bf16[1,512,2048]{2,1,0:T(8,128)(2,1)} %param.11) | copy-start | bytes 6291460
  7.2 77.1 %all-reduce.3.cloned.1.call-start = ((), (), s32[]{:S(2)}) async-start(), calls=%async_computation.2 | async-start | bytes 524288 | tf_op jit(solution)/shard_map/psum | solution.py:21
  15.3 3.9 %copy-start.6 = (f32[512,32]{0,1:T(8,128)S(1)}, f32[512,32]{0,1:T(8,128)}, u32[]{:S(2)}) copy-start(f32[512,32]{0,1:T(8,128)} %param.10) | copy-start | bytes 196612
  26.0 214.2 %all-reduce.5.cloned.1.call-start = ((), (), s32[]{:S(2)}) async-start(), calls=%async_computation.3 | async-start | bytes 524288 | tf_op jit(solution)/shard_map/psum | solution.py:27
  116.3 153.8 %all-gather.2.cloned.1.call-start = ((), (), s32[]{:S(2)}) async-start(), calls=%async_computation.1 | async-start | bytes 2359296 | tf_op jit(solution)/shard_map/all_gather | solution.py:14
  117.0 193.9 %reduce-scatter.2.cloned.1.call-start = ((), (), s32[]{:S(2)}) async-start(), calls=%async_computation.4 | async-start | bytes 1310720 | tf_op jit(solution)/shard_map/reduce_scatter | solution.py:39
  270.1 6.3 %copy-start.1 = (bf16[2048,512]{0,1:T(8,128)(2,1)S(1)}, bf16[2048,512]{0,1:T(8,128)(2,1)}, u32[]{:S(2)}) copy-start(bf16[2048,512]{0,1:T(8,128)(2,1)} %copy.10) | copy-start | bytes 6291460
  270.1 6.3 %copy-start.2 = (bf16[1,2048,512]{1,2,0:T(8,128)(2,1)S(1)}, bf16[1,2048,512]{1,2,0:T(8,128)(2,1)}, u32[]{:S(2)}) copy-start(bf16[1,2048,512]{1,2,0:T(8,128)(2,1)} %copy.11) | copy-start | bytes 6291460
  270.1 6.3 %copy-start.3 = (bf16[1,2048,512]{1,2,0:T(8,128)(2,1)S(1)}, bf16[1,2048,512]{1,2,0:T(8,128)(2,1)}, u32[]{:S(2)}) copy-start(bf16[1,2048,512]{1,2,0:T(8,128)(2,1)} %copy.12) | copy-start | bytes 6291460
  270.1 6.3 %copy-start.4 = (bf16[2048,512]{0,1:T(8,128)(2,1)S(1)}, bf16[2048,512]{0,1:T(8,128)(2,1)}, u32[]{:S(2)}) copy-start(bf16[2048,512]{0,1:T(8,128)(2,1)} %all-gather.2.cloned.1.call-done) | copy-start | bytes 6291460
  279.8 1.3 copy-start.5
Sparse Core Ops, SparseCore 0:
  26.1 58.1 all-reduce.2
  116.4 123.7 all-reduce.4
  241.8 28.1 all-gather.1
  283.6 27.3 reduce-scatter.1
where the time goes:
time: 320 us; the launch traced here: 319 us
  waiting for transfers between devices  230 us (72%)
  matrix products  24.5 us (8%)
  local copies, waits for them, and re-layouts  23.7 us (7%)
  blocking collectives  16 us (5%)
  between operations  13.8 us (4%)
  other arithmetic  11.1 us (3%)
    psum x1, waiting for transfers between devices, on_device(): q_mean = lax.psum(q_raw, ('replica', 'shard')) / replicas  123 us
    psum x1, waiting for transfers between devices, on_device(): p_mean = lax.psum(p_local, 'replica') / replicas  58.3 us
    all_gather x1, waiting for transfers between devices, on_device(): full_momentum = lax.all_gather(momentum, 'replica', axis=1, tiled=True)  29.8 us
    unnamed x20, local copies, waits for them, and re-layouts  22 us
    reduce_scatter x1, waiting for transfers between devices, on_device(): lax.psum_scatter(jnp.dot(own_tokens, new_base, preferred_element_type=jnp...  17.9 us
    psum x1, blocking collectives, on_device(): gram_sum = lax.psum(own_gram, 'shard')  16 us
    dot_general x1, matrix products, on_device(): p_local = jnp.dot(pseudo, q_start, precision=highest)  6.77 us
  transfers between devices with their start and end apart: 4, of which 4 were waited for; matrix products, arithmetic and copies ran while one was open for 3% of the time, Pallas kernels for 0%

commit v1 on v0

v1 whole, which is shorter than its diff:
```python
import functools

import jax
import jax.numpy as jnp
from jax import lax
from jax.experimental import pallas as pl
from jax.experimental.pallas import tpu as pltpu
from jax.sharding import PartitionSpec as P

outer_mu = 0.9
outer_rate = 0.7
MESH = pl.DeviceIdType.MESH
F32 = jnp.float32
BF16 = jnp.bfloat16
NT = (((1,), (1,)), ((), ()))
NN = (((1,), (0,)), ((), ()))
TN = (((0,), (0,)), ((), ()))
HIGHEST = lax.Precision.HIGHEST


def split3(x):
    high = x.astype(BF16)
    rest = x - high.astype(F32)
    mid = rest.astype(BF16)
    low = (rest - mid.astype(F32)).astype(BF16)
    return high, mid, low


def stack3(x):
    return jnp.concatenate(split3(x), axis=0)


def fold3(x):
    n = x.shape[0] // 3
    return x[:n] + (x[n : 2 * n] + x[2 * n :])


def invert(a):
    n = a.shape[0]
    rows = lax.broadcasted_iota(jnp.int32, (n, n), 0)
    cols = lax.broadcasted_iota(jnp.int32, (n, n), 1)
    lane = lax.broadcasted_iota(jnp.int32, (1, n), 1)
    for k in range(n):
        inverse_pivot = 1.0 / a[k : k + 1, k : k + 1]
        col = a[:, k : k + 1]
        row = jnp.where(lane == k, 1.0, a[k : k + 1, :]) * inverse_pivot
        a = jnp.where(rows == k, row, jnp.where(cols == k, 0.0, a) - col * row)
    return a


def exchange(cfg, lw, base, ef, qt, mom, pm_out, x_out, xo_out, slots,
             lw_v, base_v, ef_v, mom_v, pt, pair_in, half, rs_in, pm, gs, g_in,
             tl, tr_in, ts, ts_in, tt,
             ld_sem, mom_ld, pair_sem, rs_send, rs_recv, ag_send, ag_recv, fw_send,
             g_send, g_recv, tr_send, tr_recv, ts_send, ts_recv, ta_send, ta_recv,
             mr_send, ml_send, mf_send, m_recv, out_sem):
    R, S, d, kv, rank = cfg
    L = R // 2
    me = lax.axis_index("replica")
    shard = lax.axis_index("shard")
    core = lax.rem(me, 2)
    pos = me // 2
    partner = me + 1 - 2 * core
    chunks = ld_sem.shape[1]
    rows = d // chunks

    def at_replica(r):
        return {"replica": r}

    def at_shard(s):
        return {"shard": s}

    loads = []
    for k in range(chunks):
        trio = []
        for n, (src, dst) in enumerate(((lw, lw_v), (base, base_v), (ef, ef_v))):
            part = pl.ds(k * rows, rows)
            cp = pltpu.make_async_copy(src.at[part], dst.at[part], ld_sem.at[n, k])
            cp.start()
            trio.append(cp)
        loads.append(trio)
    own_in = pltpu.make_async_copy(mom, mom_v, mom_ld.at[0])
    own_in.start()

    barrier = pltpu.get_barrier_semaphore()
    for k in range(1, R):
        pl.semaphore_signal(barrier, inc=1, device_id=at_replica(lax.rem(me + k, R)), device_id_type=MESH)
    for k in range(1, S):
        pl.semaphore_signal(barrier, inc=1, device_id=at_shard(lax.rem(shard + k, S)), device_id_type=MESH)
    pl.semaphore_wait(barrier, R - 1 + S - 1)

    def rcopy(src, dst, ss, rs, dev):
        return pltpu.make_async_remote_copy(src_ref=src, dst_ref=dst, send_sem=ss, recv_sem=rs,
                                            device_id=dev, device_id_type=MESH)

    def block_of(p):
        return 2 * p + core

    def move(step, wait):
        right_origin = jnp.clip(pos - (step - 1), 0, L - 1)
        left_origin = jnp.clip(pos + (step - 1), 0, L - 1)

        def go(origin, sem, target):
            b = block_of(origin)
            src = mom_v if step == 1 else slots.at[b]
            cp = rcopy(src, slots.at[b], sem.at[step - 1], m_recv.at[b], at_replica(block_of(target)))
            cp.wait_send() if wait else cp.start()

        @pl.when((pos - (step - 1) >= 0) & (pos + 1 < L))
        def _():
            go(right_origin, mr_send, jnp.minimum(pos + 1, L - 1))

        @pl.when((pos + (step - 1) < L) & (pos >= 1))
        def _():
            go(left_origin, ml_send, jnp.maximum(pos - 1, 0))

    def forward(b, sem, src, wait):
        cp = rcopy(src, slots.at[b], sem, m_recv.at[b], at_replica(partner))
        cp.wait_send() if wait else cp.start()

    def arrived(step):
        for side, sign in enumerate((-1, 1)):
            origin = pos + sign * step

            @pl.when((origin >= 0) & (origin < L))
            def _():
                b = block_of(jnp.clip(origin, 0, L - 1))
                rcopy(slots.at[b], slots.at[b], mf_send.at[side, step - 1], m_recv.at[b], at_replica(partner)).wait_recv()
                forward(b, mf_send.at[side, step - 1], slots.at[b], False)

    own_in.wait()
    move(1, False)
    own_out = pltpu.make_async_copy(mom_v, slots.at[me], mom_ld.at[1])
    own_out.start()

    q3 = stack3(qt[...])
    for k in range(chunks):
        for cp in loads[k]:
            cp.wait()
        part = pl.ds(k * rows, rows)
        acc = lax.dot_general(q3, base_v[part, :], NT, preferred_element_type=F32)
        acc -= lax.dot_general(q3, lw_v[part, :], NT, preferred_element_type=F32)
        acc += lax.dot_general(q3, ef_v[part, :], NT, preferred_element_type=F32)
        pt[:, part] = fold3(acc)

    h = d // 2
    nc = L
    while h % nc or (h // nc) % 128:
        nc //= 2
    w = h // nc
    theirs = pl.ds(pl.multiple_of((1 - core) * h, 128), h)
    mine = pl.ds(pl.multiple_of(core * h, 128), h)
    pair = rcopy(pt.at[:, theirs], pair_in, pair_sem.at[0], pair_sem.at[1], at_replica(partner))
    pair.start()
    pair.wait_recv()
    half[...] = pt[:, mine] + pair_in[...]

    owner = pos < nc

    def when_owner(f):
        if nc == L:
            f()
        else:
            pl.when(owner)(f)

    def rs_copy(k):
        target = lax.rem(pos + k, L)
        src = half.at[:, pl.ds(pl.multiple_of(jnp.minimum(target, nc - 1) * w, 128), w)]
        return target, rcopy(src, rs_in.at[pos], rs_send.at[k], rs_recv.at[pos], at_replica(block_of(target)))

    def per_target(k, f):
        target, cp = rs_copy(k)
        if nc == L:
            f(cp)
        else:
            pl.when(target < nc)(lambda: f(cp))

    for k in range(1, L):
        per_target(k, lambda cp: cp.start())
    own_pos = jnp.minimum(pos, nc - 1)

    def cols_of(c, p):
        return pl.ds(pl.multiple_of(c * h + p * w, 128), w)

    def reduce_own():
        total = half[:, pl.ds(pl.multiple_of(own_pos * w, 128), w)]
        for k in range(1, L):
            source = lax.rem(pos + k, L)
            rcopy(rs_in.at[source], rs_in.at[source], rs_send.at[k], rs_recv.at[source], at_replica(partner)).wait_recv()
            total += rs_in[source]
        pm[:, cols_of(core, own_pos)] = total * (1.0 / R)
        for k in range(1, L):
            ag_copy(k).start()
        fw_copy(core, own_pos, fw_send.at[0]).start()

    def ag_copy(k):
        dst = pm.at[:, cols_of(core, own_pos)]
        return rcopy(dst, dst, ag_send.at[k], ag_recv.at[core, own_pos], at_replica(block_of(lax.rem(pos + k, L))))

    def fw_copy(c, p, sem):
        dst = pm.at[:, cols_of(c, p)]
        return rcopy(dst, dst, sem, ag_recv.at[c, p], at_replica(partner))

    when_owner(reduce_own)
    for k in range(1, L):
        source = lax.rem(pos + k, L)
        p = jnp.minimum(source, nc - 1)

        def take():
            fw_copy(core, p, fw_send.at[k]).wait_recv()
            fw_copy(core, p, fw_send.at[k]).start()

        if nc == L:
            take()
        else:
            pl.when(source < nc)(take)
    for p in range(nc):
        fw_copy(1 - core, p, fw_send.at[0]).wait_recv()

    whole_pm = pm[...]
    gs[...] = jnp.zeros_like(gs)
    gs[:, 0:rank] = lax.dot_general(whole_pm, whole_pm, NT, precision=HIGHEST, preferred_element_type=F32)

    def g_copy(k):
        return rcopy(gs, g_in.at[shard], g_send.at[k], g_recv.at[shard], at_shard(lax.rem(shard + k, S)))

    for k in range(1, S):
        g_copy(k).start()
    acc = None
    for k in range(chunks):
        part = pl.ds(k * rows, rows)
        p3 = stack3(pm[:, part])
        term = lax.dot_general(p3, base_v[part, :], NN, preferred_element_type=F32)
        term -= lax.dot_general(p3, lw_v[part, :], NN, preferred_element_type=F32)
        term += lax.dot_general(p3, ef_v[part, :], NN, preferred_element_type=F32)
        acc = term if acc is None else acc + term
    tl[...] = fold3(acc)

    groups = rank // 8
    tiles = min(R, groups * (kv // 128))
    wl = kv // (tiles // groups)

    def tile_of(j):
        return (pl.ds(pl.multiple_of(lax.rem(j, groups) * 8, 8), 8),
                pl.ds(pl.multiple_of((j // groups) * wl, 128), wl))

    t_owner = me < tiles

    def when_tile(cond, f):
        if tiles == R:
            f()
        else:
            pl.when(cond)(f)

    def tr_copy(k):
        target = lax.rem(me + k, R)
        a, b = tile_of(jnp.minimum(target, tiles - 1))
        return target < tiles, rcopy(tl.at[a, b], tr_in.at[me], tr_send.at[k], tr_recv.at[me], at_replica(target))

    for k in range(1, R):
        cond, cp = tr_copy(k)
        when_tile(cond, lambda cp=cp: cp.start())

    if L > 2:
        arrived(1)
        own_out.wait()
        move(2, False)
    elif L > 1:
        arrived(1)
        own_out.wait()
    else:
        own_out.wait()

    my_tile = tile_of(jnp.minimum(me, tiles - 1))

    def ts_copy(k):
        return rcopy(ts, ts_in.at[shard], ts_send.at[k], ts_recv.at[shard], at_shard(lax.rem(shard + k, S)))

    def ta_copy(k):
        dst = tt.at[my_tile[0], my_tile[1]]
        return rcopy(dst, dst, ta_send.at[k], ta_recv.at[jnp.minimum(me, tiles - 1)], at_replica(lax.rem(me + k, R)))

    def reduce_tile():
        total = tl[my_tile[0], my_tile[1]]
        for k in range(1, R):
            source = lax.rem(me + k, R)
            rcopy(tr_in.at[source], tr_in.at[source], tr_send.at[k], tr_recv.at[source], at_replica(partner)).wait_recv()
            total += tr_in[source]
        ts[...] = total
        for k in range(1, S):
            ts_copy(k).start()
        for k in range(1, S):
            source = lax.rem(shard + k, S)
            rcopy(ts_in.at[source], ts_in.at[source], ts_send.at[k], ts_recv.at[source], at_replica(partner)).wait_recv()
            total += ts_in[source]
        tt[my_tile[0], my_tile[1]] = total * (1.0 / R)
        for k in range(1, R):
            ta_copy(k).start()

    when_tile(t_owner, reduce_tile)

    for step in range(2, L):
        arrived(step)
        if step + 1 < L:
            move(step + 1, False)
    gram = gs[:, 0:rank]
    for k in range(1, S):
        source = lax.rem(shard + k, S)
        rcopy(g_in.at[source], g_in.at[source], g_send.at[k], g_recv.at[source], at_replica(partner)).wait_recv()
        gram = gram + g_in[source][:, 0:rank]
    inverse = invert(gram)

    for k in range(1, R):
        source = lax.rem(me + k, R)
        j = jnp.minimum(source, tiles - 1)
        a, b = tile_of(j)

        def got(j=j, a=a, b=b, k=k):
            rcopy(tt.at[a, b], tt.at[a, b], ta_send.at[k], ta_recv.at[j], at_replica(partner)).wait_recv()

        when_tile(source < tiles, got)
    x = lax.dot_general(inverse, tt[...], NN, precision=HIGHEST, preferred_element_type=F32)
    x_out[...] = x
    own_columns = xo_out.shape[1]
    pick = (lax.broadcasted_iota(jnp.int32, (kv, own_columns), 0)
            == me * own_columns + lax.broadcasted_iota(jnp.int32, (kv, own_columns), 1)).astype(F32)
    xo_out[...] = lax.dot_general(x, pick, NN, precision=HIGHEST, preferred_element_type=F32)
    pm_out[...] = whole_pm

    forward(me, mf_send.at[0, L - 1], mom_v, False)
    for p in range(L):
        b = 2 * p + 1 - core
        rcopy(slots.at[b], slots.at[b], mf_send.at[0, L - 1], m_recv.at[b], at_replica(partner)).wait_recv()

    forward(me, mf_send.at[0, L - 1], mom_v, True)
    pair.wait_send()
    for k in range(1, L):
        per_target(k, lambda cp: cp.wait_send())

    def drain_own():
        for k in range(1, L):
            ag_copy(k).wait_send()
        fw_copy(core, own_pos, fw_send.at[0]).wait_send()

    when_owner(drain_own)
    for k in range(1, L):
        source = lax.rem(pos + k, L)
        p = jnp.minimum(source, nc - 1)

        def drain_fw(p=p, k=k):
            fw_copy(core, p, fw_send.at[k]).wait_send()

        if nc == L:
            drain_fw()
        else:
            pl.when(source < nc)(drain_fw)
    for k in range(1, S):
        g_copy(k).wait_send()
    for k in range(1, R):
        cond, cp = tr_copy(k)
        when_tile(cond, lambda cp=cp: cp.wait_send())

    def drain_tile():
        for k in range(1, S):
            ts_copy(k).wait_send()
        for k in range(1, R):
            ta_copy(k).wait_send()

    when_tile(t_owner, drain_tile)
    for step in range(1, L):
        move(step, True)
        for side, sign in enumerate((-1, 1)):
            origin = pos + sign * step

            @pl.when((origin >= 0) & (origin < L))
            def _():
                b = block_of(jnp.clip(origin, 0, L - 1))
                forward(b, mf_send.at[side, step - 1], slots.at[b], True)


def local_step(tr, pm, x, xo, base, lw, ef, mom, slots, tokens,
               nb_out, nm_out, ne_out, kp_out, acc, x6, xo6):
    step = pl.program_id(0)

    def six_x(v):
        a, b, l = split3(v)
        return jnp.concatenate([a, b, a, l, b, a], axis=0)

    @pl.when(step == 0)
    def _():
        x6[...] = six_x(x[...])
        xo6[...] = six_x(xo[...])

    a, b, l = split3(pm[...])
    p6 = jnp.concatenate([a, a, b, a, b, l], axis=0)
    update = lax.dot_general(p6, x6[...], TN, preferred_element_type=F32)
    own_update = lax.dot_general(xo6[...], p6, TN, preferred_element_type=F32)
    nm_out[...] = (outer_mu * mom[...].astype(F32) + own_update).astype(BF16)
    base32 = base[...].astype(F32)
    ne_out[...] = ((base32 - lw[...].astype(F32) + ef[...].astype(F32)) - update).astype(BF16)
    full = slots[...].reshape(-1, tr).astype(F32).T
    moment = outer_mu * full + update
    nb = (base32 - outer_rate * (outer_mu * moment + update)).astype(BF16)
    nb_out[...] = nb
    term = jnp.dot(tokens[...], nb, preferred_element_type=F32)

    @pl.when(step == 0)
    def _():
        acc[...] = term

    @pl.when(step > 0)
    def _():
        acc[...] += term

    @pl.when(step == pl.num_programs(0) - 1)
    def _():
        kp_out[...] = acc[...].astype(BF16)


def key_scatter(S, kp, out, own, inbox, ld_sem, send, recv):
    shard = lax.axis_index("shard")
    n = out.shape[0]

    def part(s):
        return pl.ds(pl.multiple_of(s * n, 16), n)

    ld = pltpu.make_async_copy(kp.at[part(shard)], own, ld_sem)
    ld.start()
    barrier = pltpu.get_barrier_semaphore()
    for k in range(1, S):
        pl.semaphore_signal(barrier, inc=1, device_id={"shard": lax.rem(shard + k, S)}, device_id_type=MESH)
    pl.semaphore_wait(barrier, S - 1)

    def cp(k):
        target = lax.rem(shard + k, S)
        return pltpu.make_async_remote_copy(
            src_ref=kp.at[part(target)], dst_ref=inbox.at[shard], send_sem=send.at[k],
            recv_sem=recv.at[shard], device_id={"shard": target}, device_id_type=MESH)

    for k in range(1, S):
        cp(k).start()
    ld.wait()
    total = own[...].astype(F32)
    for k in range(1, S):
        source = lax.rem(shard + k, S)
        pltpu.make_async_remote_copy(
            src_ref=inbox.at[source], dst_ref=inbox.at[source], send_sem=send.at[k],
            recv_sem=recv.at[source], device_id={"shard": source}, device_id_type=MESH).wait_recv()
        total += inbox[source].astype(F32)
    out[...] = total.astype(BF16)
    for k in range(1, S):
        cp(k).wait_send()


def on_device(local_weights, outer_base, momentum, error_feedback, q_start, tokens):
    R = lax.axis_size("replica")
    S = lax.axis_size("shard")
    d, kv = outer_base.shape
    rank = q_start.shape[1]
    c = momentum.shape[1]
    L = R // 2
    lw, ef, tok = local_weights[0], error_feedback[0], tokens[0]
    nt = tok.shape[0]
    mom_t = momentum.T
    any_spec = pl.BlockSpec(memory_space=pl.ANY)
    vm = pl.BlockSpec(memory_space=pltpu.VMEM)
    chunks = min(4, d // 128)
    h = d // 2
    nc = L
    while h % nc or (h // nc) % 128:
        nc //= 2
    w = h // nc
    tiles = min(R, (rank // 8) * (kv // 128))
    wl = kv // (tiles // (rank // 8))
    V = pltpu.VMEM
    dma = pltpu.SemaphoreType.DMA
    pm, x, xo, slots = pl.pallas_call(
        functools.partial(exchange, (R, S, d, kv, rank)),
        out_shape=(
            jax.ShapeDtypeStruct((rank, d), F32),
            jax.ShapeDtypeStruct((rank, kv), F32),
            jax.ShapeDtypeStruct((rank, c), F32),
            jax.ShapeDtypeStruct((R, c, d), BF16),
        ),
        in_specs=[any_spec, any_spec, any_spec, vm, any_spec],
        out_specs=(vm, vm, vm, any_spec),
        scratch_shapes=[
            V((d, kv), BF16), V((d, kv), BF16), V((d, kv), BF16), V((c, d), BF16),
            V((rank, d), F32), V((rank, h), F32), V((rank, h), F32), V((L, rank, w), F32), V((rank, d), F32),
            V((rank, 128), F32), V((S, rank, 128), F32),
            V((rank, kv), F32), V((R, 8, wl), F32), V((8, wl), F32), V((S, 8, wl), F32), V((rank, kv), F32),
            dma((3, chunks)), dma((2,)), dma((2,)), dma((L,)), dma((L,)), dma((L,)), dma((2, L)), dma((L,)),
            dma((S,)), dma((S,)), dma((R,)), dma((R,)), dma((S,)), dma((S,)), dma((R,)), dma((R,)),
            dma((L,)), dma((L,)), dma((2, L)), dma((R,)), dma((1,)),
        ],
        compiler_params=pltpu.CompilerParams(collective_id=0, has_side_effects=True),
        name="exchange",
    )(lw, outer_base, ef, q_start.T, mom_t)

    tr = 256
    row = lambda i: (i, 0)
    nb, nm, ne, kp = pl.pallas_call(
        functools.partial(local_step, tr),
        grid=(d // tr,),
        out_shape=(
            jax.ShapeDtypeStruct((d, kv), BF16),
            jax.ShapeDtypeStruct((c, d), BF16),
            jax.ShapeDtypeStruct((d, kv), BF16),
            jax.ShapeDtypeStruct((nt, kv), BF16),
        ),
        in_specs=[
            pl.BlockSpec((rank, tr), lambda i: (0, i)),
            pl.BlockSpec((rank, kv), lambda i: (0, 0)),
            pl.BlockSpec((rank, c), lambda i: (0, 0)),
            pl.BlockSpec((tr, kv), row),
            pl.BlockSpec((tr, kv), row),
            pl.BlockSpec((tr, kv), row),
            pl.BlockSpec((c, tr), lambda i: (0, i)),
            pl.BlockSpec((R, c, tr), lambda i: (0, 0, i)),
            pl.BlockSpec((nt, tr), lambda i: (0, i)),
        ],
        out_specs=(
            pl.BlockSpec((tr, kv), row),
            pl.BlockSpec((c, tr), lambda i: (0, i)),
            pl.BlockSpec((tr, kv), row),
            pl.BlockSpec((nt, kv), lambda i: (0, 0)),
        ),
        scratch_shapes=[V((nt, kv), F32), V((6 * rank, kv), BF16), V((6 * rank, c), BF16)],
        compiler_params=pltpu.CompilerParams(dimension_semantics=("arbitrary",)),
        name="local_step",
    )(pm, x, xo, outer_base, lw, ef, mom_t, slots, tok)

    n = nt // S
    keys = pl.pallas_call(
        functools.partial(key_scatter, S),
        out_shape=jax.ShapeDtypeStruct((n, kv), BF16),
        in_specs=[any_spec],
        out_specs=vm,
        scratch_shapes=[V((n, kv), BF16), V((S, n, kv), BF16), dma(()), dma((S,)), dma((S,))],
        compiler_params=pltpu.CompilerParams(collective_id=1, has_side_effects=True),
        name="key_scatter",
    )(kp)
    return nb, nm.T, ne[None], keys[None]


def solution(mesh):
    in_specs = (
        P("replica", "shard", None),
        P("shard", None),
        P("shard", "replica"),
        P("replica", "shard", None),
        P(),
        P("replica", None, "shard"),
    )
    out_specs = (
        P("shard", None),
        P("shard", "replica"),
        P("replica", "shard", None),
        P("replica", "shard", None),
    )
    return jax.shard_map(
        on_device, mesh=mesh, in_specs=in_specs, out_specs=out_specs, check_vma=False
    )
```

time: 320 us -> 70.5 us (0.22)
  waiting for transfers between devices: 230 us -> 0 us
  Pallas kernels: 0 us -> 67.9 us
  matrix products: 24.5 us -> 0 us
  local copies, waits for them, and re-layouts: 23.7 us -> 1.57 us
  blocking collectives: 16 us -> 0 us
  between operations: 13.8 us -> 0.65 us
  other arithmetic: 11.1 us -> 0 us
    psum x2 -> x0, waiting for transfers between devices: 181 us -> none  [the longest x1 123 us: on_device(): q_mean = lax.psum(q_raw, ('replica', 'shard')) / replicas]
    pallas_call x0 -> x3, Pallas kernels: none -> 67.9 us  [the longest x1 45.9 us: on_device(): pl.pallas_call(functools.partial(exchange, (R, S, d, kv, rank)), out_shap...]
    all_gather x1 -> x0, waiting for transfers between devices: 29.8 us -> none  [on_device(): full_momentum = lax.all_gather(momentum, 'replica', axis=1, tiled=True)]
    dot_general x5 -> x0, matrix products: 23.1 us -> none  [the longest x1 6.77 us: on_device(): p_local = jnp.dot(pseudo, q_start, precision=highest)]
    unnamed x20 -> x1, local copies, waits for them, and re-layouts: 22 us -> 1.57 us
    reduce_scatter x1 -> x0, waiting for transfers between devices: 17.9 us -> none  [on_device(): lax.psum_scatter(jnp.dot(own_tokens, new_base, preferred_element_type=jnp...]
    psum x1 -> x0, blocking collectives: 16 us -> none  [on_device(): gram_sum = lax.psum(own_gram, 'shard')]
    another operation x5 -> x0, other arithmetic: 6.68 us -> none  [the longest x3 3.59 us: on_device(): factor_low = jnp.linalg.cholesky(gram_sum)]
  transfers between devices with their start and end apart: 4 -> 0, of which waited for: 4 -> 0; matrix products, arithmetic and copies ran while one was open for 3% -> 0% of each run, Pallas kernels for 0% -> 0%
where the time goes in v1:
time: 70.5 us; the launch traced here: 70.1 us
  Pallas kernels  67.9 us (96%)
  local copies, waits for them, and re-layouts  1.57 us (2%)
    pallas_call x1, Pallas kernels, on_device(): pl.pallas_call(functools.partial(exchange, (R, S, d, kv, rank)), out_shap...  45.9 us
    pallas_call x1, Pallas kernels, on_device(): pl.pallas_call(functools.partial(local_step, tr), grid=(d // tr,), out_sh...  11.5 us
    pallas_call x1, Pallas kernels, on_device(): pl.pallas_call(functools.partial(key_scatter, S), out_shape=jax.ShapeDtyp...  10.5 us
    unnamed x1, local copies, waits for them, and re-layouts  1.57 us

profile of v1, /device:TPU:0, one launch (start us, length us, event | category | flops | bytes accessed | tf_op | source)
XLA Modules:
  0.0 70.1 jit_solution(5644153372996864161)
XLA Ops:
  0.6 45.9 %exchange.1 = (f32[32,2048]{1,0:T(8,128)}, f32[32,512]{1,0:T(8,128)}, f32[32,64]{1,0:T(8,128)}, bf16[8,64,2048]{2,1,0:T(8,128)(2,1)}) custom-call(bf16[2048,512]{1,0:T(8,128)(2,1)} %bitcast.8, bf16[2048,512]{1,0:T(8,128)(2,1)} %base.3, bf16[2048,512]{1,0:T(8,128)(2,1)} %bitcast.10, f32[32,512]{1,0:T(8,128)} %bitcast.16, bf16[64,2048]{1,0:T(8,128)(2,1)} %bitcast.13), custom_call_target="tpu_custom_call" | custom-call | tf_op jit(solution)/shard_map/exchange/pallas_call | solution.py:477
  46.6 11.5 %local_step.1 = (bf16[2048,512]{1,0:T(8,128)(2,1)}, bf16[64,2048]{1,0:T(8,128)(2,1)}, bf16[2048,512]{1,0:T(8,128)(2,1)}, bf16[512,512]{1,0:T(8,128)(2,1)}) custom-call(f32[32,2048]{1,0:T(8,128)} %get-tuple-element.12.pm, f32[32,512]{1,0:T(8,128)} %get-tuple-element.13.x, f32[32,64]{1,0:T(8,128)} %get-tuple-element.14.xo, bf16[2048,512]{1,0:T(8,128)(2,1)} %base.3, ...), custom_call_target="tpu_custom_call" | custom-call | tf_op jit(solution)/shard_map/local_step/pallas_call | solution.py:502
  58.1 10.5 %key_scatter.1 = bf16[128,512]{1,0:T(8,128)(2,1)} custom-call(bf16[512,512]{1,0:T(8,128)(2,1)} %get-tuple-element.19.kp), custom_call_target="tpu_custom_call" | custom-call | tf_op jit(solution)/shard_map/key_scatter/pallas_call | solution.py:534
  68.5 1.6 %copy.11 = bf16[1,128,512]{2,1,0:T(8,128)(2,1)} copy(bf16[1,128,512]{2,1,0:T(8,128)(2,1)} %bitcast.15) | data formatting | bytes 262144

commit v2 on v1

--- a/solution.py
+++ b/solution.py
@@ -48,12 +48,13 @@
     return a
 
 
-def exchange(cfg, lw, base, ef, qt, mom, pm_out, x_out, xo_out, slots,
-             lw_v, base_v, ef_v, mom_v, pt, pair_in, half, rs_in, pm, gs, g_in,
+def exchange(cfg, lw, base, ef, qt, mom, tok, pm_out, x_out, xo_out, a_out, b_out, mom_out,
+             lw_v, base_v, ef_v, tok_v, slots, mom_rows, pt, pair_in, half, rs_in, pm, gs, g_in,
              tl, tr_in, ts, ts_in, tt,
              ld_sem, mom_ld, pair_sem, rs_send, rs_recv, ag_send, ag_recv, fw_send,
              g_send, g_recv, tr_send, tr_recv, ts_send, ts_recv, ta_send, ta_recv,
-             mr_send, ml_send, mf_send, m_recv, out_sem):
+             mr_send, ml_send, mf_send, m_recv, out_sem,
+             a_buf, a_bf, a_in, bt, b_in, a_send, a_recv, b_send, b_recv):
     R, S, d, kv, rank = cfg
     L = R // 2
     me = lax.axis_index("replica")
@@ -79,8 +80,10 @@
             cp.start()
             trio.append(cp)
         loads.append(trio)
-    own_in = pltpu.make_async_copy(mom, mom_v, mom_ld.at[0])
+    own_in = pltpu.make_async_copy(mom, slots.at[me], mom_ld.at[0])
     own_in.start()
+    tok_in = pltpu.make_async_copy(tok, tok_v, mom_ld.at[1])
+    tok_in.start()
 
     barrier = pltpu.get_barrier_semaphore()
     for k in range(1, R):
@@ -102,8 +105,7 @@
 
         def go(origin, sem, target):
             b = block_of(origin)
-            src = mom_v if step == 1 else slots.at[b]
-            cp = rcopy(src, slots.at[b], sem.at[step - 1], m_recv.at[b], at_replica(block_of(target)))
+            cp = rcopy(slots.at[b], slots.at[b], sem.at[step - 1], m_recv.at[b], at_replica(block_of(target)))
             cp.wait_send() if wait else cp.start()
 
         @pl.when((pos - (step - 1) >= 0) & (pos + 1 < L))
@@ -130,8 +132,58 @@
 
     own_in.wait()
     move(1, False)
-    own_out = pltpu.make_async_copy(mom_v, slots.at[me], mom_ld.at[1])
-    own_out.start()
+    forward(me, mf_send.at[0, L - 1], slots.at[me], False)
+
+    c = slots.shape[1]
+    per = 128 // c
+    blocks = kv // 128
+    n = tok.shape[0] // S
+    early = per == 2
+
+    def token_rows(s):
+        return pl.ds(pl.multiple_of(s * n, 128), n)
+
+    def block_cols(bk):
+        return pl.ds(pl.multiple_of(bk * 128, 128), 128)
+
+    def a_copy(k, bk):
+        target = lax.rem(shard + k, S)
+        return rcopy(a_bf.at[token_rows(target), block_cols(bk)], a_in.at[shard, :, block_cols(bk)],
+                     a_send.at[k, bk], a_recv.at[shard, bk], at_shard(target))
+
+    def mom_copy(bk):
+        return pltpu.make_async_copy(mom_rows.at[:, block_cols(bk)], mom_out.at[:, block_cols(bk)], out_sem.at[bk])
+
+    def key_block(bk):
+        cols = block_cols(bk)
+        block = slots[pl.ds(bk * per, per)].reshape(128, d)
+        a = a_buf[:, cols] - (outer_rate * outer_mu * outer_mu) * lax.dot_general(
+            tok_v[...], block, NT, preferred_element_type=F32)
+        a_buf[:, cols] = a
+        a_bf[:, cols] = a.astype(BF16)
+        for k in range(1, S):
+            a_copy(k, bk).start()
+        mom_rows[:, cols] = block.T
+        mom_copy(bk).start()
+
+    def partner_block(p):
+        b = 2 * p + 1 - core
+        rcopy(slots.at[b], slots.at[b], mf_send.at[0, L - 1], m_recv.at[b], at_replica(partner)).wait_recv()
+
+    def blocks_at(step):
+        def side(i, carry):
+            origin = pos + (2 * i - 1) * step
+
+            @pl.when((origin >= 0) & (origin < L))
+            def _():
+                p = jnp.clip(origin, 0, L - 1)
+                partner_block(p)
+                if early:
+                    key_block(p)
+
+            return carry
+
+        lax.fori_loop(0, 2, side, 0)
 
     q3 = stack3(qt[...])
     for k in range(chunks):
@@ -152,6 +204,8 @@
     mine = pl.ds(pl.multiple_of(core * h, 128), h)
     pair = rcopy(pt.at[:, theirs], pair_in, pair_sem.at[0], pair_sem.at[1], at_replica(partner))
     pair.start()
+    tok_in.wait()
+    a_buf[...] = jnp.dot(tok_v[...], base_v[...], preferred_element_type=F32)
     pair.wait_recv()
     half[...] = pt[:, mine] + pair_in[...]
 
@@ -177,6 +231,9 @@
 
     for k in range(1, L):
         per_target(k, lambda cp: cp.start())
+    partner_block(pos)
+    if early:
+        key_block(pos)
     own_pos = jnp.minimum(pos, nc - 1)
 
     def cols_of(c, p):
@@ -202,6 +259,8 @@
         return rcopy(dst, dst, sem, ag_recv.at[c, p], at_replica(partner))
 
     when_owner(reduce_own)
+    if L > 1:
+        arrived(1)
     for k in range(1, L):
         source = lax.rem(pos + k, L)
         p = jnp.minimum(source, nc - 1)
@@ -217,15 +276,6 @@
     for p in range(nc):
         fw_copy(1 - core, p, fw_send.at[0]).wait_recv()
 
-    whole_pm = pm[...]
-    gs[...] = jnp.zeros_like(gs)
-    gs[:, 0:rank] = lax.dot_general(whole_pm, whole_pm, NT, precision=HIGHEST, preferred_element_type=F32)
-
-    def g_copy(k):
-        return rcopy(gs, g_in.at[shard], g_send.at[k], g_recv.at[shard], at_shard(lax.rem(shard + k, S)))
-
-    for k in range(1, S):
-        g_copy(k).start()
     acc = None
     for k in range(chunks):
         part = pl.ds(k * rows, rows)
@@ -262,14 +312,30 @@
         when_tile(cond, lambda cp=cp: cp.start())
 
     if L > 2:
-        arrived(1)
-        own_out.wait()
         move(2, False)
-    elif L > 1:
-        arrived(1)
-        own_out.wait()
-    else:
-        own_out.wait()
+
+    whole_pm = pm[...]
+    gs[...] = jnp.zeros_like(gs)
+    gs[:, 0:rank] = lax.dot_general(whole_pm, whole_pm, NT, precision=HIGHEST, preferred_element_type=F32)
+
+    def g_copy(k):
+        return rcopy(gs, g_in.at[shard], g_send.at[k], g_recv.at[shard], at_shard(lax.rem(shard + k, S)))
+
+    for k in range(1, S):
+        g_copy(k).start()
+    b_acc = None
+    for k in range(chunks):
+        part = pl.ds(k * rows, rows)
+        term = lax.dot_general(stack3(pm[:, part]), tok_v[:, part], NT, preferred_element_type=F32)
+        b_acc = term if b_acc is None else b_acc + term
+    bt[...] = fold3(b_acc)
+
+    def b_copy(k):
+        target = lax.rem(shard + k, S)
+        return rcopy(bt.at[:, token_rows(target)], b_in.at[shard], b_send.at[k], b_recv.at[shard], at_shard(target))
+
+    for k in range(1, S):
+        b_copy(k).start()
 
     my_tile = tile_of(jnp.minimum(me, tiles - 1))
 
@@ -280,7 +346,7 @@
         dst = tt.at[my_tile[0], my_tile[1]]
         return rcopy(dst, dst, ta_send.at[k], ta_recv.at[jnp.minimum(me, tiles - 1)], at_replica(lax.rem(me + k, R)))
 
-    def reduce_tile():
+    def reduce_replicas():
         total = tl[my_tile[0], my_tile[1]]
         for k in range(1, R):
             source = lax.rem(me + k, R)
@@ -289,6 +355,9 @@
         ts[...] = total
         for k in range(1, S):
             ts_copy(k).start()
+
+    def reduce_shards():
+        total = ts[...]
         for k in range(1, S):
             source = lax.rem(shard + k, S)
             rcopy(ts_in.at[source], ts_in.at[source], ts_send.at[k], ts_recv.at[source], at_replica(partner)).wait_recv()
@@ -297,18 +366,29 @@
         for k in range(1, R):
             ta_copy(k).start()
 
-    when_tile(t_owner, reduce_tile)
-
-    for step in range(2, L):
-        arrived(step)
-        if step + 1 < L:
-            move(step + 1, False)
+    when_tile(t_owner, reduce_replicas)
+    if L > 1:
+        blocks_at(1)
+    when_tile(t_owner, reduce_shards)
+
+    if L > 2:
+        arrived(2)
+        if L > 3:
+            move(3, False)
+
     gram = gs[:, 0:rank]
     for k in range(1, S):
         source = lax.rem(shard + k, S)
         rcopy(g_in.at[source], g_in.at[source], g_send.at[k], g_recv.at[source], at_replica(partner)).wait_recv()
         gram = gram + g_in[source][:, 0:rank]
     inverse = invert(gram)
+    for step in range(2, L):
+        if step > 2:
+            arrived(step)
+            if step + 1 < L:
+                move(step + 1, False)
+        if step < L - 1:
+            blocks_at(step)
 
     for k in range(1, R):
         source = lax.rem(me + k, R)
@@ -325,14 +405,37 @@
     pick = (lax.broadcasted_iota(jnp.int32, (kv, own_columns), 0)
             == me * own_columns + lax.broadcasted_iota(jnp.int32, (kv, own_columns), 1)).astype(F32)
     xo_out[...] = lax.dot_general(x, pick, NN, precision=HIGHEST, preferred_element_type=F32)
-    pm_out[...] = whole_pm
-
-    forward(me, mf_send.at[0, L - 1], mom_v, False)
-    for p in range(L):
-        b = 2 * p + 1 - core
-        rcopy(slots.at[b], slots.at[b], mf_send.at[0, L - 1], m_recv.at[b], at_replica(partner)).wait_recv()
-
-    forward(me, mf_send.at[0, L - 1], mom_v, True)
+    pm_out[...] = pm[...]
+
+    if L > 2:
+        blocks_at(L - 1)
+    if not early:
+        def late(bk, carry):
+            key_block(bk)
+            return carry
+
+        lax.fori_loop(0, blocks, late, 0)
+
+    total = a_buf[token_rows(shard), :]
+    b_total = bt[:, token_rows(shard)]
+    for k in range(1, S):
+        source = lax.rem(shard + k, S)
+        for bk in range(blocks):
+            part = a_in.at[source, :, block_cols(bk)]
+            rcopy(part, part, a_send.at[k, bk], a_recv.at[source, bk], at_replica(partner)).wait_recv()
+        total += a_in[source].astype(F32)
+        rcopy(b_in.at[source], b_in.at[source], b_send.at[k], b_recv.at[source], at_replica(partner)).wait_recv()
+        b_total += b_in[source]
+    a_out[...] = total
+    b_out[...] = b_total
+    for bk in range(blocks):
+        mom_copy(bk).wait()
+
+    forward(me, mf_send.at[0, L - 1], slots.at[me], True)
+    for k in range(1, S):
+        for bk in range(blocks):
+            a_copy(k, bk).wait_send()
+        b_copy(k).wait_send()
     pair.wait_send()
     for k in range(1, L):
         per_target(k, lambda cp: cp.wait_send())
@@ -378,8 +481,8 @@
                 forward(b, mf_send.at[side, step - 1], slots.at[b], True)
 
 
-def local_step(tr, pm, x, xo, base, lw, ef, mom, slots, tokens,
-               nb_out, nm_out, ne_out, kp_out, acc, x6, xo6):
+def local_step(tr, pm, x, xo, a_own, b_own, base, lw, ef, mom, mom_rows,
+               nb_out, nm_out, ne_out, key_out, x6, xo6):
     step = pl.program_id(0)
 
     def six_x(v):
@@ -390,6 +493,8 @@
     def _():
         x6[...] = six_x(x[...])
         xo6[...] = six_x(xo[...])
+        key_out[...] = (a_own[...] - (outer_rate * (outer_mu + 1.0)) * lax.dot_general(
+            b_own[...], x[...], TN, precision=HIGHEST, preferred_element_type=F32)).astype(BF16)
 
     a, b, l = split3(pm[...])
     p6 = jnp.concatenate([a, a, b, a, b, l], axis=0)
@@ -398,58 +503,8 @@
     nm_out[...] = (outer_mu * mom[...].astype(F32) + own_update).astype(BF16)
     base32 = base[...].astype(F32)
     ne_out[...] = ((base32 - lw[...].astype(F32) + ef[...].astype(F32)) - update).astype(BF16)
-    full = slots[...].reshape(-1, tr).astype(F32).T
-    moment = outer_mu * full + update
-    nb = (base32 - outer_rate * (outer_mu * moment + update)).astype(BF16)
-    nb_out[...] = nb
-    term = jnp.dot(tokens[...], nb, preferred_element_type=F32)
-
-    @pl.when(step == 0)
-    def _():
-        acc[...] = term
-
-    @pl.when(step > 0)
-    def _():
-        acc[...] += term
-
-    @pl.when(step == pl.num_programs(0) - 1)
-    def _():
-        kp_out[...] = acc[...].astype(BF16)
-
-
-def key_scatter(S, kp, out, own, inbox, ld_sem, send, recv):
-    shard = lax.axis_index("shard")
-    n = out.shape[0]
-
-    def part(s):
-        return pl.ds(pl.multiple_of(s * n, 16), n)
-
-    ld = pltpu.make_async_copy(kp.at[part(shard)], own, ld_sem)
-    ld.start()
-    barrier = pltpu.get_barrier_semaphore()
-    for k in range(1, S):
-        pl.semaphore_signal(barrier, inc=1, device_id={"shard": lax.rem(shard + k, S)}, device_id_type=MESH)
-    pl.semaphore_wait(barrier, S - 1)
-
-    def cp(k):
-        target = lax.rem(shard + k, S)
-        return pltpu.make_async_remote_copy(
-            src_ref=kp.at[part(target)], dst_ref=inbox.at[shard], send_sem=send.at[k],
-            recv_sem=recv.at[shard], device_id={"shard": target}, device_id_type=MESH)
-
-    for k in range(1, S):
-        cp(k).start()
-    ld.wait()
-    total = own[...].astype(F32)
-    for k in range(1, S):
-        source = lax.rem(shard + k, S)
-        pltpu.make_async_remote_copy(
-            src_ref=inbox.at[source], dst_ref=inbox.at[source], send_sem=send.at[k],
-            recv_sem=recv.at[source], device_id={"shard": source}, device_id_type=MESH).wait_recv()
-        total += inbox[source].astype(F32)
-    out[...] = total.astype(BF16)
-    for k in range(1, S):
-        cp(k).wait_send()
+    moment = outer_mu * mom_rows[...].astype(F32) + update
+    nb_out[...] = (base32 - outer_rate * (outer_mu * moment + update)).astype(BF16)
 
 
 def on_device(local_weights, outer_base, momentum, error_feedback, q_start, tokens):
@@ -474,72 +529,68 @@
     wl = kv // (tiles // (rank // 8))
     V = pltpu.VMEM
     dma = pltpu.SemaphoreType.DMA
-    pm, x, xo, slots = pl.pallas_call(
+    n = nt // S
+    pm, x, xo, a_own, b_own, mom_rows = pl.pallas_call(
         functools.partial(exchange, (R, S, d, kv, rank)),
         out_shape=(
             jax.ShapeDtypeStruct((rank, d), F32),
             jax.ShapeDtypeStruct((rank, kv), F32),
             jax.ShapeDtypeStruct((rank, c), F32),
-            jax.ShapeDtypeStruct((R, c, d), BF16),
+            jax.ShapeDtypeStruct((n, kv), F32),
+            jax.ShapeDtypeStruct((rank, n), F32),
+            jax.ShapeDtypeStruct((d, kv), BF16),
         ),
-        in_specs=[any_spec, any_spec, any_spec, vm, any_spec],
-        out_specs=(vm, vm, vm, any_spec),
+        in_specs=[any_spec, any_spec, any_spec, vm, any_spec, any_spec],
+        out_specs=(vm, vm, vm, vm, vm, any_spec),
         scratch_shapes=[
-            V((d, kv), BF16), V((d, kv), BF16), V((d, kv), BF16), V((c, d), BF16),
+            V((d, kv), BF16), V((d, kv), BF16), V((d, kv), BF16), V((nt, d), BF16), V((R, c, d), BF16), V((d, kv), BF16),
             V((rank, d), F32), V((rank, h), F32), V((rank, h), F32), V((L, rank, w), F32), V((rank, d), F32),
             V((rank, 128), F32), V((S, rank, 128), F32),
             V((rank, kv), F32), V((R, 8, wl), F32), V((8, wl), F32), V((S, 8, wl), F32), V((rank, kv), F32),
             dma((3, chunks)), dma((2,)), dma((2,)), dma((L,)), dma((L,)), dma((L,)), dma((2, L)), dma((L,)),
             dma((S,)), dma((S,)), dma((R,)), dma((R,)), dma((S,)), dma((S,)), dma((R,)), dma((R,)),
-            dma((L,)), dma((L,)), dma((2, L)), dma((R,)), dma((1,)),
+            dma((L,)), dma((L,)), dma((2, L)), dma((R,)), dma((kv // 128,)),
+            V((nt, kv), F32), V((nt, kv), BF16), V((S, n, kv), BF16), V((rank, nt), F32), V((S, rank, n), F32),
+            dma((S, kv // 128)), dma((S, kv // 128)), dma((S,)), dma((S,)),
         ],
         compiler_params=pltpu.CompilerParams(collective_id=0, has_side_effects=True),
         name="exchange",
-    )(lw, outer_base, ef, q_start.T, mom_t)
+    )(lw, outer_base, ef, q_start.T, mom_t, tok)
 
     tr = 256
     row = lambda i: (i, 0)
-    nb, nm, ne, kp = pl.pallas_call(
+    nb, nm, ne, keys = pl.pallas_call(
         functools.partial(local_step, tr),
         grid=(d // tr,),
         out_shape=(
             jax.ShapeDtypeStruct((d, kv), BF16),
             jax.ShapeDtypeStruct((c, d), BF16),
             jax.ShapeDtypeStruct((d, kv), BF16),
-            jax.ShapeDtypeStruct((nt, kv), BF16),
+            jax.ShapeDtypeStruct((n, kv), BF16),
         ),
         in_specs=[
             pl.BlockSpec((rank, tr), lambda i: (0, i)),
             pl.BlockSpec((rank, kv), lambda i: (0, 0)),
             pl.BlockSpec((rank, c), lambda i: (0, 0)),
+            pl.BlockSpec((n, kv), lambda i: (0, 0)),
+            pl.BlockSpec((rank, n), lambda i: (0, 0)),
             pl.BlockSpec((tr, kv), row),
             pl.BlockSpec((tr, kv), row),
             pl.BlockSpec((tr, kv), row),
             pl.BlockSpec((c, tr), lambda i: (0, i)),
-            pl.BlockSpec((R, c, tr), lambda i: (0, 0, i)),
-            pl.BlockSpec((nt, tr), lambda i: (0, i)),
+            pl.BlockSpec((tr, kv), row),
         ],
         out_specs=(
             pl.BlockSpec((tr, kv), row),
             pl.BlockSpec((c, tr), lambda i: (0, i)),
             pl.BlockSpec((tr, kv), row),
-            pl.BlockSpec((nt, kv), lambda i: (0, 0)),
+            pl.BlockSpec((n, kv), lambda i: (0, 0)),
         ),
-        scratch_shapes=[V((nt, kv), F32), V((6 * rank, kv), BF16), V((6 * rank, c), BF16)],
+        scratch_shapes=[V((6 * rank, kv), BF16), V((6 * rank, c), BF16)],
         compiler_params=pltpu.CompilerParams(dimension_semantics=("arbitrary",)),
         name="local_step",
-    )(pm, x, xo, outer_base, lw, ef, mom_t, slots, tok)
-
-    n = nt // S
-    keys = pl.pallas_call(
-        functools.partial(key_scatter, S),
-        out_shape=jax.ShapeDtypeStruct((n, kv), BF16),
-        in_specs=[any_spec],
-        out_specs=vm,
-        scratch_shapes=[V((n, kv), BF16), V((S, n, kv), BF16), dma(()), dma((S,)), dma((S,))],
-        compiler_params=pltpu.CompilerParams(collective_id=1, has_side_effects=True),
-        name="key_scatter",
-    )(kp)
+    )(pm, x, xo, a_own, b_own, outer_base, lw, ef, mom_t, mom_rows)
+
     return nb, nm.T, ne[None], keys[None]
 
 

time: 70.5 us -> 58.7 us (0.83)
  Pallas kernels: 67.9 us -> 57.7 us
  local copies, waits for them, and re-layouts: 1.57 us -> 0 us
    pallas_call x1 -> x0, Pallas kernels: 10.5 us -> none  [on_device(): pl.pallas_call(functools.partial(key_scatter, S), out_shape=jax.ShapeDtyp...]
    pallas_call x1, Pallas kernels: 45.9 us -> 48 us  [on_device(): pl.pallas_call(functools.partial(exchange, (R, S, d, kv, rank)), out_shap...]
    pallas_call x1, Pallas kernels: 11.5 us -> 9.68 us  [on_device(): pl.pallas_call(functools.partial(local_step, tr), grid=(d // tr,), out_sh...]
    unnamed x1 -> x0, local copies, waits for them, and re-layouts: 1.57 us -> none
where the time goes in v2:
time: 58.7 us; the launch traced here: 58.3 us
  Pallas kernels  57.7 us (98%)
  between operations  0.64 us (1%)
    pallas_call x1, Pallas kernels, on_device(): pl.pallas_call(functools.partial(exchange, (R, S, d, kv, rank)), out_shap...  48 us
    pallas_call x1, Pallas kernels, on_device(): pl.pallas_call(functools.partial(local_step, tr), grid=(d // tr,), out_sh...  9.68 us

profile of v2, /device:TPU:0, one launch (start us, length us, event | category | flops | bytes accessed | tf_op | source)
XLA Modules:
  0.0 58.3 jit_solution(15476106750752932183)
XLA Ops:
  0.6 48.0 %exchange.1 = (f32[32,2048]{1,0:T(8,128)}, f32[32,512]{1,0:T(8,128)}, f32[32,64]{1,0:T(8,128)}, f32[128,512]{1,0:T(8,128)}, f32[32,128]{1,0:T(8,128)}, /*index=5*/bf16[2048,512]{1,0:T(8,128)(2,1)}) custom-call(bf16[2048,512]{1,0:T(8,128)(2,1)} %bitcast.8, bf16[2048,512]{1,0:T(8,128)(2,1)} %base.3, bf16[2048,512]{1,0:T(8,128)(2,1)} %bitcast.10, ...), custom_call_target="tpu_custom_call" | custom-call | tf_op jit(solution)/shard_map/exchange/pallas_call | solution.py:533
  48.6 9.7 %local_step.1 = (bf16[2048,512]{1,0:T(8,128)(2,1)}, bf16[64,2048]{1,0:T(8,128)(2,1)}, bf16[2048,512]{1,0:T(8,128)(2,1)}, bf16[128,512]{1,0:T(8,128)(2,1)}) custom-call(f32[32,2048]{1,0:T(8,128)} %get-tuple-element.14.pm, f32[32,512]{1,0:T(8,128)} %get-tuple-element.15.x, f32[32,64]{1,0:T(8,128)} %get-tuple-element.16.xo, ...), custom_call_target="tpu_custom_call" | custom-call | tf_op jit(solution)/shard_map/local_step/pallas_call | solution.py:562

commit v3 on v2

--- a/solution.py
+++ b/solution.py
@@ -99,13 +99,19 @@
     def block_of(p):
         return 2 * p + core
 
-    def move(step, wait):
+    HV = 2
+    span = d // HV
+
+    def slot(b, hv):
+        return slots.at[b, :, pl.ds(hv * span, span)]
+
+    def move(step, hv, wait):
         right_origin = jnp.clip(pos - (step - 1), 0, L - 1)
         left_origin = jnp.clip(pos + (step - 1), 0, L - 1)
 
         def go(origin, sem, target):
             b = block_of(origin)
-            cp = rcopy(slots.at[b], slots.at[b], sem.at[step - 1], m_recv.at[b], at_replica(block_of(target)))
+            cp = rcopy(slot(b, hv), slot(b, hv), sem.at[step - 1, hv], m_recv.at[b, hv], at_replica(block_of(target)))
             cp.wait_send() if wait else cp.start()
 
         @pl.when((pos - (step - 1) >= 0) & (pos + 1 < L))
@@ -116,23 +122,27 @@
         def _():
             go(left_origin, ml_send, jnp.maximum(pos - 1, 0))
 
-    def forward(b, sem, src, wait):
-        cp = rcopy(src, slots.at[b], sem, m_recv.at[b], at_replica(partner))
+    def forward(b, side, index, hv, wait):
+        cp = rcopy(slot(b, hv), slot(b, hv), mf_send.at[side, index, hv], m_recv.at[b, hv], at_replica(partner))
         cp.wait_send() if wait else cp.start()
 
-    def arrived(step):
+    def await_half(b, hv):
+        rcopy(slot(b, hv), slot(b, hv), mf_send.at[0, 0, hv], m_recv.at[b, hv], at_replica(partner)).wait_recv()
+
+    def arrived(step, hv):
         for side, sign in enumerate((-1, 1)):
             origin = pos + sign * step
 
             @pl.when((origin >= 0) & (origin < L))
             def _():
                 b = block_of(jnp.clip(origin, 0, L - 1))
-                rcopy(slots.at[b], slots.at[b], mf_send.at[side, step - 1], m_recv.at[b], at_replica(partner)).wait_recv()
-                forward(b, mf_send.at[side, step - 1], slots.at[b], False)
+                await_half(b, hv)
+                forward(b, side, step - 1, hv, False)
 
     own_in.wait()
-    move(1, False)
-    forward(me, mf_send.at[0, L - 1], slots.at[me], False)
+    for hv in range(HV):
+        move(1, hv, False)
+        forward(me, 0, L - 1, hv, False)
 
     c = slots.shape[1]
     per = 128 // c
@@ -166,9 +176,15 @@
         mom_rows[:, cols] = block.T
         mom_copy(bk).start()
 
+    def advance(step, hv):
+        if step < L:
+            arrived(step, hv)
+        if step + 1 < L:
+            move(step + 1, hv, False)
+
     def partner_block(p):
-        b = 2 * p + 1 - core
-        rcopy(slots.at[b], slots.at[b], mf_send.at[0, L - 1], m_recv.at[b], at_replica(partner)).wait_recv()
+        for hv in range(HV):
+            await_half(2 * p + 1 - core, hv)
 
     def blocks_at(step):
         def side(i, carry):
@@ -234,6 +250,7 @@
     partner_block(pos)
     if early:
         key_block(pos)
+    advance(1, 0)
     own_pos = jnp.minimum(pos, nc - 1)
 
     def cols_of(c, p):
@@ -259,8 +276,8 @@
         return rcopy(dst, dst, sem, ag_recv.at[c, p], at_replica(partner))
 
     when_owner(reduce_own)
-    if L > 1:
-        arrived(1)
+    for hv in range(1, HV):
+        advance(1, hv)
     for k in range(1, L):
         source = lax.rem(pos + k, L)
         p = jnp.minimum(source, nc - 1)
@@ -311,8 +328,7 @@
         cond, cp = tr_copy(k)
         when_tile(cond, lambda cp=cp: cp.start())
 
-    if L > 2:
-        move(2, False)
+    advance(2, 0)
 
     whole_pm = pm[...]
     gs[...] = jnp.zeros_like(gs)
@@ -367,14 +383,14 @@
             ta_copy(k).start()
 
     when_tile(t_owner, reduce_replicas)
+    for hv in range(1, HV):
+        advance(2, hv)
     if L > 1:
         blocks_at(1)
     when_tile(t_owner, reduce_shards)
 
-    if L > 2:
-        arrived(2)
-        if L > 3:
-            move(3, False)
+    if 2 < L - 1:
+        blocks_at(2)
 
     gram = gs[:, 0:rank]
     for k in range(1, S):
@@ -382,11 +398,9 @@
         rcopy(g_in.at[source], g_in.at[source], g_send.at[k], g_recv.at[source], at_replica(partner)).wait_recv()
         gram = gram + g_in[source][:, 0:rank]
     inverse = invert(gram)
-    for step in range(2, L):
-        if step > 2:
-            arrived(step)
-            if step + 1 < L:
-                move(step + 1, False)
+    for step in range(3, L):
+        for hv in range(HV):
+            advance(step, hv)
         if step < L - 1:
             blocks_at(step)
 
@@ -431,7 +445,8 @@
     for bk in range(blocks):
         mom_copy(bk).wait()
 
-    forward(me, mf_send.at[0, L - 1], slots.at[me], True)
+    for hv in range(HV):
+        forward(me, 0, L - 1, hv, True)
     for k in range(1, S):
         for bk in range(blocks):
             a_copy(k, bk).wait_send()
@@ -471,14 +486,14 @@
 
     when_tile(t_owner, drain_tile)
     for step in range(1, L):
-        move(step, True)
-        for side, sign in enumerate((-1, 1)):
-            origin = pos + sign * step
-
-            @pl.when((origin >= 0) & (origin < L))
-            def _():
-                b = block_of(jnp.clip(origin, 0, L - 1))
-                forward(b, mf_send.at[side, step - 1], slots.at[b], True)
+        for hv in range(HV):
+            move(step, hv, True)
+            for side, sign in enumerate((-1, 1)):
+                origin = pos + sign * step
+
+                @pl.when((origin >= 0) & (origin < L))
+                def _():
+                    forward(block_of(jnp.clip(origin, 0, L - 1)), side, step - 1, hv, True)
 
 
 def local_step(tr, pm, x, xo, a_own, b_own, base, lw, ef, mom, mom_rows,
@@ -549,7 +564,7 @@
             V((rank, kv), F32), V((R, 8, wl), F32), V((8, wl), F32), V((S, 8, wl), F32), V((rank, kv), F32),
             dma((3, chunks)), dma((2,)), dma((2,)), dma((L,)), dma((L,)), dma((L,)), dma((2, L)), dma((L,)),
             dma((S,)), dma((S,)), dma((R,)), dma((R,)), dma((S,)), dma((S,)), dma((R,)), dma((R,)),
-            dma((L,)), dma((L,)), dma((2, L)), dma((R,)), dma((kv // 128,)),
+            dma((L, 2)), dma((L, 2)), dma((2, L, 2)), dma((R, 2)), dma((kv // 128,)),
             V((nt, kv), F32), V((nt, kv), BF16), V((S, n, kv), BF16), V((rank, nt), F32), V((S, rank, n), F32),
             dma((S, kv // 128)), dma((S, kv // 128)), dma((S,)), dma((S,)),
         ],
@@ -557,7 +572,7 @@
         name="exchange",
     )(lw, outer_base, ef, q_start.T, mom_t, tok)
 
-    tr = 256
+    tr = min(512, d)
     row = lambda i: (i, 0)
     nb, nm, ne, keys = pl.pallas_call(
         functools.partial(local_step, tr),

time: 58.7 us -> 52.7 us (0.90)
  Pallas kernels: 57.7 us -> 51.8 us
    pallas_call x1, Pallas kernels: 48 us -> 43.9 us  [on_device(): pl.pallas_call(functools.partial(exchange, (R, S, d, kv, rank)), out_shap...]
    pallas_call x1, Pallas kernels: 9.68 us -> 7.86 us  [on_device(): pl.pallas_call(functools.partial(local_step, tr), grid=(d // tr,), out_sh...]
where the time goes in v3:
time: 52.7 us; the launch traced here: 52.4 us
  Pallas kernels  51.8 us (98%)
  between operations  0.64 us (1%)
    pallas_call x1, Pallas kernels, on_device(): pl.pallas_call(functools.partial(exchange, (R, S, d, kv, rank)), out_shap...  43.9 us
    pallas_call x1, Pallas kernels, on_device(): pl.pallas_call(functools.partial(local_step, tr), grid=(d // tr,), out_sh...  7.86 us

profile of v3, /device:TPU:0, one launch (start us, length us, event | category | flops | bytes accessed | tf_op | source)
XLA Modules:
  0.0 52.4 jit_solution(2684556298700122914)
XLA Ops:
  0.6 43.9 %exchange.1 = (f32[32,2048]{1,0:T(8,128)}, f32[32,512]{1,0:T(8,128)}, f32[32,64]{1,0:T(8,128)}, f32[128,512]{1,0:T(8,128)}, f32[32,128]{1,0:T(8,128)}, /*index=5*/bf16[2048,512]{1,0:T(8,128)(2,1)}) custom-call(bf16[2048,512]{1,0:T(8,128)(2,1)} %bitcast.8, bf16[2048,512]{1,0:T(8,128)(2,1)} %base.3, bf16[2048,512]{1,0:T(8,128)(2,1)} %bitcast.10, ...), custom_call_target="tpu_custom_call" | custom-call | tf_op jit(solution)/shard_map/exchange/pallas_call | solution.py:548
  44.6 7.9 %local_step.1 = (bf16[2048,512]{1,0:T(8,128)(2,1)}, bf16[64,2048]{1,0:T(8,128)(2,1)}, bf16[2048,512]{1,0:T(8,128)(2,1)}, bf16[128,512]{1,0:T(8,128)(2,1)}) custom-call(f32[32,2048]{1,0:T(8,128)} %get-tuple-element.14.pm, f32[32,512]{1,0:T(8,128)} %get-tuple-element.15.x, f32[32,64]{1,0:T(8,128)} %get-tuple-element.16.xo, ...), custom_call_target="tpu_custom_call" | custom-call | tf_op jit(solution)/shard_map/local_step/pallas_call | solution.py:577

commit v4 on v3

--- a/solution.py
+++ b/solution.py
@@ -572,7 +572,7 @@
         name="exchange",
     )(lw, outer_base, ef, q_start.T, mom_t, tok)
 
-    tr = min(512, d)
+    tr = min(1024, d)
     row = lambda i: (i, 0)
     nb, nm, ne, keys = pl.pallas_call(
         functools.partial(local_step, tr),

time: 52.7 us -> 52 us (0.987)
  Pallas kernels: 51.8 us -> 51.2 us
    pallas_call x1, Pallas kernels: 7.86 us -> 7.24 us  [on_device(): pl.pallas_call(functools.partial(local_step, tr), grid=(d // tr,), out_sh...]
where the time goes in v4:
time: 52 us; the launch traced here: 51.8 us
  Pallas kernels  51.2 us (98%)
  between operations  0.64 us (1%)
    pallas_call x1, Pallas kernels, on_device(): pl.pallas_call(functools.partial(exchange, (R, S, d, kv, rank)), out_shap...  43.9 us
    pallas_call x1, Pallas kernels, on_device(): pl.pallas_call(functools.partial(local_step, tr), grid=(d // tr,), out_sh...  7.24 us

profile of v4, /device:TPU:0, one launch (start us, length us, event | category | flops | bytes accessed | tf_op | source)
XLA Modules:
  0.0 51.8 jit_solution(10564314828470081064)
XLA Ops:
  0.6 43.9 %exchange.1 = (f32[32,2048]{1,0:T(8,128)}, f32[32,512]{1,0:T(8,128)}, f32[32,64]{1,0:T(8,128)}, f32[128,512]{1,0:T(8,128)}, f32[32,128]{1,0:T(8,128)}, /*index=5*/bf16[2048,512]{1,0:T(8,128)(2,1)}) custom-call(bf16[2048,512]{1,0:T(8,128)(2,1)} %bitcast.8, bf16[2048,512]{1,0:T(8,128)(2,1)} %base.3, bf16[2048,512]{1,0:T(8,128)(2,1)} %bitcast.10, ...), custom_call_target="tpu_custom_call" | custom-call | tf_op jit(solution)/shard_map/exchange/pallas_call | solution.py:548
  44.6 7.2 %local_step.1 = (bf16[2048,512]{1,0:T(8,128)(2,1)}, bf16[64,2048]{1,0:T(8,128)(2,1)}, bf16[2048,512]{1,0:T(8,128)(2,1)}, bf16[128,512]{1,0:T(8,128)(2,1)}) custom-call(f32[32,2048]{1,0:T(8,128)} %get-tuple-element.14.pm, f32[32,512]{1,0:T(8,128)} %get-tuple-element.15.x, f32[32,64]{1,0:T(8,128)} %get-tuple-element.16.xo, ...), custom_call_target="tpu_custom_call" | custom-call | tf_op jit(solution)/shard_map/local_step/pallas_call | solution.py:577
